TPU v7x, 32 devices: a whole 2x2x4 slice. The times are simulated.
32 devices in a mesh: rows: 2 (over core), waves: 16 (over z, y, x).
Axes of the slice: x: 2, y: 2, z: 4, core: 2. Of those that a mesh axis runs over, the one named last changes fastest.
Arguments:
- feats: float32 [8192, 256], P(('rows', 'waves')), may hold values from -6 to 6
- positions: float32 [3, 8192], P(None, ('rows', 'waves')), may hold values from 0 to 6
- cell_counts: int32 [64], P(('rows', 'waves')), may hold values from 1 to 128
- neighbours: int32 [64, 5], P(('rows', 'waves')), may hold values from 0 to 63, as said below
- nbr_count: int32 [64], P(('rows', 'waves')), may hold values from 3 to 5
- kvec: float32 [3, 3072], P(None, 'waves'), may hold values from -4 to 4
- filters: float32 [3072, 256], P('waves'), may hold values from -5 to 5
- w_msg: float32 [256, 256], replicated, may hold values from -0.375 to 0.375
- w_val: float32 [256, 256], replicated, may hold values from -0.375 to 0.375
- w_one: float32 [256, 256], replicated, may hold values from -0.375 to 0.375
- w_two: float32 [256, 256], replicated, may hold values from -0.375 to 0.375
Outputs:
- updated: float32 [8192, 256], P(('rows', 'waves'))
Inputs may be any that keep to these rules, and one draw needn't show every extreme that they name: `neighbours`: column 0 of each cell's list is the cell itself, column 1 the cell (c - 2) mod 64, column 2 the cell (c + 2) mod 64; the 5 entries of a list are distinct cells, and every listed cell c' of cell c satisfies (c' - c) mod 64 <= 2 or (c - c') mod 64 <= 2; entries at or beyond nbr_count are in range and unused.
All inputs are finite; a program needn't handle non-finite values.
Results may differ from a plain program's by a relative error of at most 0.0003.
Values sent between devices are 32-bit elements; how exact they have to be, the bound alone decides.
A program may use at most 128 MiB of HBM per device.

v0:
```python
import math

import jax
import jax.numpy as jnp
from jax import lax
from jax.sharding import PartitionSpec as P

HIGH = lax.Precision.HIGHEST


def extended(cells, sides, width):
    for axis, dim in sides:
        count = lax.axis_size(axis)
        head = lax.slice_in_dim(cells, 0, width, axis=dim)
        tail = lax.slice_in_dim(cells, cells.shape[dim] - width, cells.shape[dim], axis=dim)
        cells = jnp.concatenate(
            [
                lax.ppermute(tail, axis, [(i, (i + 1) % count) for i in range(count)]),
                cells,
                lax.ppermute(head, axis, [((i + 1) % count, i) for i in range(count)]),
            ],
            axis=dim,
        )
    return cells


def shards(
    feats, positions, cell_counts, neighbours, nbr_count, kvec, filters, w_msg, w_val, w_one, w_two
):
    cells = cell_counts.shape[0]
    slots = feats.shape[0]
    cell = slots // cells
    width = feats.shape[1]
    kcol = kvec.shape[1]
    devices = lax.axis_size("rows") * lax.axis_size("waves")
    slot_ids = jnp.arange(cell, dtype=jnp.int32)
    valid2 = (slot_ids[None, :] < cell_counts[:, None]).astype(jnp.float32)
    valid = valid2.reshape(-1)
    hw_cols = jnp.einsum("fg,sf->gs", w_msg, feats, precision=HIGH)
    payload = jnp.concatenate([hw_cols, positions, valid[None, :]], axis=0)
    widened = extended(payload, ((("rows", "waves"), 1),), slots)
    widened = widened.reshape(width + 4, 3 * cells, cell)
    first = lax.axis_index(("rows", "waves")) * cells
    total_cells = cells * devices
    own_ids = first + jnp.arange(cells, dtype=jnp.int32)
    own_pos = positions.reshape(3, cells, cell)
    same_slot = jnp.eye(cell, dtype=jnp.bool_)
    msg0 = jnp.zeros((cells, cell, width), jnp.float32)
    msg = msg0
    for index in range(neighbours.shape[1]):
        listed = lax.dynamic_index_in_dim(neighbours, index, 1, keepdims=False)
        local = (listed - first + cells) % total_cells
        blocks = jnp.take(widened, local, axis=1)
        near_hw = blocks[:width]
        near_pos = blocks[width : width + 3]
        near_valid = blocks[width + 3]
        dist = jnp.sum((own_pos[:, :, :, None] - near_pos[:, :, None, :]) ** 2, axis=0)
        live = (index < nbr_count).astype(jnp.float32)
        keep = valid2[:, :, None] * near_valid[:, None, :] * live[:, None, None]
        same = (listed == own_ids)[:, None, None] & same_slot[None]
        weight = jnp.where(same, 0.0, jnp.exp(-0.125 * dist) * keep)
        msg = msg + jnp.einsum("cij,gcj->cig", weight, near_hw, precision=HIGH)
    msg = 0.125 * msg.reshape(slots, width)
    row_pos = lax.all_gather(positions, "waves", axis=1, tiled=True)
    val_cols = jnp.einsum("fg,sf->gs", w_val, feats, precision=HIGH) * valid[None, :]
    piece = lax.all_gather(val_cols, "waves", axis=1, tiled=True)
    part_pos = row_pos
    phase = jnp.dot(kvec.T, part_pos, precision=HIGH)
    dims = (((1,), (1,)), ((), ()))
    sum_cos = lax.dot_general(jnp.cos(phase), piece, dims, precision=HIGH)
    sum_sin = lax.dot_general(jnp.sin(phase), piece, dims, precision=HIGH)
    share = kcol // lax.axis_size("rows")
    part_cos, part_sin = (
        lax.psum_scatter(sum_cos, "rows", scatter_dimension=0, tiled=True),
        lax.psum_scatter(sum_sin, "rows", scatter_dimension=0, tiled=True),
    )
    filt_part = lax.dynamic_slice_in_dim(filters, lax.axis_index("rows") * share, share, 0)
    filt_cos, filt_sin = (
        lax.all_gather(part_cos * filt_part, "rows", axis=0, tiled=True),
        lax.all_gather(part_sin * filt_part, "rows", axis=0, tiled=True),
    )
    scale_factor = 1.0 / math.sqrt(float(slots * devices) * float(kcol * lax.axis_size("waves")))
    part_pos = row_pos
    phase = jnp.dot(part_pos.T, kvec, precision=HIGH)
    ewald = (
        lax.psum_scatter(
            jnp.dot(jnp.cos(phase), filt_cos, precision=HIGH)
            + jnp.dot(jnp.sin(phase), filt_sin, precision=HIGH),
            "waves",
            scatter_dimension=0,
            tiled=True,
        )
        * scale_factor
    )
    summed = feats + msg + ewald
    normed = summed / jnp.sqrt(jnp.mean(summed * summed, axis=1, keepdims=True) + 1e-06)
    hidden = jax.nn.silu(jnp.dot(normed, w_one, precision=HIGH))
    return (summed + jnp.dot(hidden, w_two, precision=HIGH)) * valid[:, None]


def solution(mesh):
    placed = (
        P(("rows", "waves"), None),
        P(None, ("rows", "waves")),
        P(("rows", "waves")),
        P(("rows", "waves"), None),
        P(("rows", "waves")),
        P(None, "waves"),
        P("waves", None),
        P(),
        P(),
        P(),
        P(),
    )
    return jax.shard_map(
        shards, mesh=mesh, in_specs=placed, out_specs=P(("rows", "waves"), None), check_vma=False
    )
```

profile of v0, /device:TPU:0, one launch (start us, length us, event | category | flops | bytes accessed | tf_op | source)
XLA Modules:
  0.0 301.3 jit_solution(16643961812289834076)
XLA Ops:
  6.5 0.8 compare_convert_fusion.5
  7.3 0.2 copy-done
  7.5 2.2 convolution_multiply_fusion
  9.8 0.0 reduce-scatter.6.cloned.1.call-start
  9.8 43.4 %all_gather.12 = f32[3,4096]{1,0:T(4,128)S(1)} all-gather(f32[3,256]{1,0:T(4,128)} %param.14), channel_id=1, replica_groups=mesh['rows'=2,'waves'=16] {'waves'}, dimensions={1}, use_global_device_ids=true | all-gather | bytes 52224 | tf_op jit(solution)/shard_map/all_gather | solution.py:64
  53.2 3.4 %fusion.120 = f32[192,4096]{1,0:T(8,128)S(1)} fusion(f32[3,192]{1,0:T(4,128)} %param.18, f32[3,4096]{1,0:T(4,128)S(1)} %all_gather.12), kind=kOutput, calls=%fused_computation.191 | convolution fusion | flops 28311552 | bytes 3197184 | tf_op jit(solution)/shard_map/dot_general | solution.py:68
  56.6 37.1 %all-gather.2.cloned.1.call-done = f32[256,4096]{1,0:T(8,128)} async-done(((f32[256,256]{1,0:T(8,128)}), f32[256,4096]{1,0:T(8,128)}) %all-gather.2.cloned.1.call-update) | async-done | bytes 4194320 | tf_op jit(solution)/shard_map/all_gather | solution.py:66
  93.7 28.3 %fusion = f32[192,256]{1,0:T(8,128)} fusion(f32[256,4096]{1,0:T(8,128)} %all-gather.2.cloned.1.call-done, f32[192,4096]{1,0:T(8,128)S(1)} %fusion.120), kind=kOutput, calls=%fused_computation.6 | convolution fusion | flops 2415919104 | bytes 7536640 | tf_op jit(solution)/shard_map/dot_general | solution.py:71
  122.1 16.7 %fusion.3 = f32[192,256]{1,0:T(8,128)} fusion(f32[256,4096]{1,0:T(8,128)} %all-gather.2.cloned.1.call-done, f32[192,4096]{1,0:T(8,128)S(1)} %fusion.120), kind=kOutput, calls=%fused_computation.9 | convolution fusion | flops 2415919104 | bytes 7536640 | tf_op jit(solution)/shard_map/dot_general | solution.py:70
  138.8 0.0 reduce-scatter.8.cloned.1.call-start
  138.9 2.7 fusion.119
  141.6 3.2 %reduce-scatter.4.cloned.1.call-done = f32[96,256]{1,0:T(8,128)} async-done(((f32[192,256]{1,0:T(8,128)}), f32[96,256]{1,0:T(8,128)}) %reduce-scatter.4.cloned.1.call-update) | async-done | bytes 98320 | tf_op jit(solution)/shard_map/reduce_scatter | solution.py:74
  144.8 1.0 dynamic-slice_multiply_fusion
  145.8 1.9 all_gather.14
  147.8 1.9 all_gather.15
  149.7 19.4 %fusion.5 = f32[4096,256]{1,0:T(8,128)S(1)} fusion(f32[192,256]{1,0:T(8,128)S(1)} %all_gather.14, f32[4096,192]{0,1:T(8,128)S(1)} %fusion.119), kind=kOutput, calls=%fused_computation.11 | convolution fusion | flops 2415919104 | bytes 7536640 | tf_op jit(solution)/shard_map/dot_general | solution.py:87
  169.2 18.6 %convolution_add_fusion = f32[4096,256]{1,0:T(8,128)} fusion(f32[4096,256]{1,0:T(8,128)S(1)} %fusion.5, f32[192,256]{1,0:T(8,128)S(1)} %all_gather.15, f32[4096,192]{0,1:T(8,128)S(1)} %fusion.119), kind=kOutput, calls=%fused_computation.5 | convolution fusion | flops 2416967680 | bytes 11730944 | tf_op jit(solution)/shard_map/dot_general | solution.py:88
  187.8 0.9 copy-done.1
  188.7 0.1 copy-done.2
  188.8 0.6 fusion.118
  189.4 5.3 %collective-permute-start.1 = (f32[260,256]{1,0:T(8,128)S(1)}, f32[260,256]{1,0:T(8,128)S(1)}, u32[]{:S(2)}, u32[]{:S(2)}) collective-permute-start(f32[260,256]{1,0:T(8,128)S(1)} %pad_maximum_fusion.1), channel_id=1, source_target_pairs={{1,0},{2,1},{3,2},{4,3},{5,4},{6,5},{7,6},{8,7},{9,8},{10,9},{11,1... | collective-permute-start | bytes 798728 | tf_op jit(solution)/shard_map/ppermute | solution.py:20
  194.8 0.2 collective-permute-start
  195.0 0.3 slice_reduce_fusion
  195.5 9.1 %collective-permute-done.1 = f32[260,256]{1,0:T(8,128)S(1)} collective-permute-done((f32[260,256]{1,0:T(8,128)S(1)}, f32[260,256]{1,0:T(8,128)S(1)}, u32[]{:S(2)}, u32[]{:S(2)}) %collective-permute-start.1) | collective-permute-done | bytes 266272 | tf_op jit(solution)/shard_map/ppermute | solution.py:20
  204.6 14.0 %collective-permute-done = f32[260,256]{1,0:T(8,128)S(1)} collective-permute-done((f32[260,256]{1,0:T(8,128)S(1)}, f32[260,256]{1,0:T(8,128)S(1)}, u32[]{:S(2)}, u32[]{:S(2)}) %collective-permute-start) | collective-permute-done | bytes 266272 | tf_op jit(solution)/shard_map/ppermute | solution.py:18
  218.6 0.1 pad_maximum_fusion
  218.6 0.1 reshape.146
  218.8 0.2 copy.27
  218.9 0.6 gather_fusion
  219.5 0.1 select_bitcast_fusion.4
  219.6 0.6 gather_fusion.1
  220.2 0.1 select_bitcast_fusion.3
  220.3 0.6 gather_fusion.2
  220.9 0.1 select_bitcast_fusion.2
  221.0 0.6 gather_fusion.3
  221.6 0.1 select_bitcast_fusion.1
  221.7 0.6 gather_fusion.4
  222.3 0.1 select_bitcast_fusion
  222.4 0.3 multiply_reduce_fusion
  222.7 0.4 fusion.13
  223.1 0.4 convolution_add_fusion.5
  223.6 0.4 convolution_add_fusion.4
  224.0 0.4 convolution_add_fusion.3
  224.4 0.4 fusion.8
  224.9 66.8 %reduce-scatter.8.cloned.1.call-done = f32[256,256]{1,0:T(8,128)} async-done(((f32[4096,256]{1,0:T(8,128)}), f32[256,256]{1,0:T(8,128)}) %reduce-scatter.8.cloned.1.call-update) | async-done | bytes 262160 | tf_op jit(solution)/shard_map/reduce_scatter | solution.py:86
  291.6 1.1 multiply_reduce_fusion.5
  292.7 0.4 fusion.21
  293.2 1.1 fusion.7
  (49 shorter events, 0.4 us)
Async XLA Ops:
  6.5 1.0 copy-start
  6.5 87.1 %all-gather.2.cloned.1.call-start = ((), (), s32[]{:S(2)}) async-start(), calls=%async_computation.3 | async-start | bytes 4456448 | tf_op jit(solution)/shard_map/all_gather | solution.py:66
  9.8 131.8 %reduce-scatter.6.cloned.1.call-start = ((), (), s32[]{:S(2)}) async-start(), calls=%async_computation.5 | async-start | bytes 294912 | tf_op jit(solution)/shard_map/reduce_scatter | solution.py:75
  122.0 16.9 %copy-start.5 = (f32[3,192]{1,0:T(4,128)S(1)}, f32[3,192]{1,0:T(4,128)}, u32[]{:S(2)}) copy-start(f32[3,192]{1,0:T(4,128)} %param.18) | copy-start | bytes 6916
  122.0 22.8 %reduce-scatter.4.cloned.1.call-start = ((), (), s32[]{:S(2)}) async-start(), calls=%async_computation.4 | async-start | bytes 294912 | tf_op jit(solution)/shard_map/reduce_scatter | solution.py:74
  138.8 152.8 %reduce-scatter.8.cloned.1.call-start = ((), (), s32[]{:S(2)}) async-start(), calls=%async_computation.6 | async-start | bytes 4456448 | tf_op jit(solution)/shard_map/reduce_scatter | solution.py:86
  187.8 0.9 copy-start.1
  187.8 1.0 copy-start.2
  187.8 1.6 copy-start.3
  187.8 7.3 %copy-start.4 = (s32[2,5]{1,0:T(2,128)S(1)}, s32[2,5]{1,0:T(2,128)}, u32[]{:S(2)}) copy-start(s32[2,5]{1,0:T(2,128)} %param.16) | copy-start | bytes 124
  187.8 7.5 %copy-start.6 = (s32[2]{0:T(128)S(1)}, s32[2]{0:T(128)}, u32[]{:S(2)}) copy-start(s32[2]{0:T(128)} %param.17) | copy-start | bytes 28
  189.4 15.1 %collective-permute-start.1 = (f32[260,256]{1,0:T(8,128)S(1)}, f32[260,256]{1,0:T(8,128)S(1)}, u32[]{:S(2)}, u32[]{:S(2)}) collective-permute-start(f32[260,256]{1,0:T(8,128)S(1)} %pad_maximum_fusion.1), channel_id=1, source_target_pairs={{1,0},{2,1},{3,2},{4,3},{5,4},{6,5},{7,6},{8,7},{9,8},{10,9},{11,1... | collective-permute-start | bytes 798728 | tf_op jit(solution)/shard_map/ppermute | solution.py:20
  194.8 23.8 %collective-permute-start = (f32[260,256]{1,0:T(8,128)S(1)}, f32[260,256]{1,0:T(8,128)S(1)}, u32[]{:S(2)}, u32[]{:S(2)}) collective-permute-start(f32[260,256]{1,0:T(8,128)S(1)} %pad_maximum_fusion.1), channel_id=1, source_target_pairs={{0,1},{1,2},{2,3},{3,4},{4,5},{5,6},{6,7},{7,8},{8,9},{9,10},{10,1... | collective-permute-start | bytes 798728 | tf_op jit(solution)/shard_map/ppermute | solution.py:18
  222.4 70.4 %copy-start.7 = (f32[256,256]{1,0:T(8,128)S(1)}, f32[256,256]{1,0:T(8,128)}, u32[]{:S(2)}) copy-start(f32[256,256]{1,0:T(8,128)} %param.22) | copy-start | bytes 786436
  222.7 70.5 %copy-start.8 = (f32[256,256]{1,0:T(8,128)S(1)}, f32[256,256]{1,0:T(8,128)}, u32[]{:S(2)}) copy-start(f32[256,256]{1,0:T(8,128)} %param.23) | copy-start | bytes 786436
Sparse Core Ops, SparseCore 0:
  10.1 83.5 all-gather.1
  122.1 5.8 reduce-scatter.5
  138.9 5.8 reduce-scatter.3
  187.9 103.6 reduce-scatter.7
where the time goes:
time: 305 us; the launch traced here: 301 us
  waiting for transfers between devices  130 us (43%)
  matrix products  95.7 us (31%)
  blocking collectives  47.2 us (15%)
  between operations  14 us (5%)
  starting transfers between devices  5.71 us (2%)
  local copies, waits for them, and re-layouts  4.64 us (2%)
  other arithmetic  3.74 us (1%)
    reduce_scatter x1, waiting for transfers between devices, shards(): lax.psum_scatter(jnp.dot(jnp.cos(phase), filt_cos, precision=HIGH) + jnp....  66.8 us
    all_gather x1, blocking collectives, shards(): row_pos = lax.all_gather(positions, 'waves', axis=1, tiled=True)  43.4 us
    all_gather x1, waiting for transfers between devices, shards(): piece = lax.all_gather(val_cols, 'waves', axis=1, tiled=True)  37.1 us
    dot_general x1, matrix products, shards(): sum_sin = lax.dot_general(jnp.sin(phase), piece, dims, precision=HIGH)  28.3 us
    dot_general x1, matrix products, shards(): jnp.dot(jnp.cos(phase), filt_cos, precision=HIGH)  19.4 us
    dot_general x1, matrix products, shards(): jnp.dot(jnp.sin(phase), filt_sin, precision=HIGH)  18.6 us
    dot_general x1, matrix products, shards(): sum_cos = lax.dot_general(jnp.cos(phase), piece, dims, precision=HIGH)  16.7 us
    ppermute x1, waiting for transfers between devices, extended(): lax.ppermute(tail, axis, [(i, (i + 1) % count) for i in range(count)])  14 us
  transfers between devices with their start and end apart: 6, of which 5 were waited for; matrix products, arithmetic and copies ran while one was open for 10% of the time, Pallas kernels for 0%

commit v1 on v0

v1 whole, which is shorter than its diff:
```python
import functools
import math

import jax
import jax.numpy as jnp
from jax import lax
from jax.experimental import pallas as pl
from jax.experimental.pallas import tpu as pltpu
from jax.sharding import PartitionSpec as P

MESH = pl.DeviceIdType.MESH
F32 = jnp.float32
BF16 = jnp.bfloat16

SIN = (6.283185302511498, -41.341700405316864, 81.60513138577438, -76.7030153535419, 42.02592698387571, -14.899846661980089, 3.238137503130986)
COS = (0.9999999890590201, -19.739204499453688, 64.93911745988827, -85.45013953077586, 60.16763095018129, -25.96759924584206, 6.528658157862129)


def split(x):
    high = x.astype(BF16)
    return high, (x - high.astype(F32)).astype(BF16)


def mm(a, b):
    return jnp.dot(a, b, preferred_element_type=F32)


def dot3(a, b):
    return mm(a[0], b[0]) + mm(a[0], b[1]) + mm(a[1], b[0])


def sincos(turns):
    x = turns - jnp.floor(turns + 0.5)
    y = x * x
    s = jnp.full_like(y, SIN[-1])
    for coefficient in SIN[-2::-1]:
        s = s * y + coefficient
    c = jnp.full_like(y, COS[-1])
    for coefficient in COS[-2::-1]:
        c = c * y + coefficient
    return s * x, c


def columns(rows):
    height, width = rows.shape
    return jnp.concatenate([rows, jnp.zeros((128 - height, width), F32)], axis=0).T


def body(
    nz, plane, scale,
    counts, neigh, ncount, feats, pos, kv, filt, w_msg, w_val, w_one, w_two,
    out,
    feats_all, pos_all, kv_all, k_cols, ch, cl, sh, sl, fbh, fbl,
    s_acc, xbuf, zs, zr, f_all, fth, ftl, es, er, msg,
    s_pos, r_pos, s_feat, r_feat, s_kv, r_kv, s_x, r_x, s_z, r_z, s_f, r_f, s_g, s_e, r_e,
):
    slots, width = feats.shape
    kb = filt.shape[0]
    half = kb // 2
    kall = nz * kb
    kpad = k_cols.shape[0]
    cells = counts.shape[0]
    cell = slots // cells
    waves = nz * plane
    r = lax.axis_index("rows")
    w = lax.axis_index("waves")
    z = w // plane
    p = w % plane
    other = (1 - r, w)
    at_low = p == 0
    at_high = p == plane - 1
    edge_w = jnp.where(at_low, (w + waves - 1) % waves, (w + 1) % waves)
    crosses = jnp.where(at_low, z == 0, z == nz - 1)
    edge_r = jnp.where(crosses, 1 - r, r)
    edge = (edge_r, edge_w)

    def plane_dev(j):
        return (r, z * plane + (p + j) % plane)

    def z_dev(j):
        return (r, ((z + j) % nz) * plane + p)

    def rcopy(src, dst, ssem, rsem, dev):
        return pltpu.make_async_remote_copy(
            src_ref=src, dst_ref=dst, send_sem=ssem, recv_sem=rsem, device_id=dev, device_id_type=MESH
        )

    def rows_of(block):
        return pl.ds(pl.multiple_of(block * slots, slots), slots)

    barrier = pltpu.get_barrier_semaphore()
    pl.semaphore_signal(barrier, inc=1, device_id=other, device_id_type=MESH)
    for j in range(1, nz):
        pl.semaphore_signal(barrier, inc=1, device_id=z_dev(j), device_id_type=MESH)

    @pl.loop(1, plane)
    def _(j):
        pl.semaphore_signal(barrier, inc=1, device_id=plane_dev(j), device_id_type=MESH)

    @pl.when(at_low | at_high)
    def _():
        pl.semaphore_signal(barrier, inc=1, device_id=edge, device_id_type=MESH)

    pl.semaphore_wait(barrier, nz + plane - 1 + jnp.where(at_low | at_high, 1, 0))

    def kv_copy(j):
        return rcopy(kv, kv_all.at[z], s_kv.at[j], r_kv.at[z], z_dev(j))

    def kv_arrival(j):
        q = (z + j) % nz
        return rcopy(kv, kv_all.at[q], s_kv.at[j], r_kv.at[q], z_dev(j))

    def pos_copy(j):
        return rcopy(pos, pos_all.at[p], s_pos.at[j], r_pos.at[p], plane_dev(j))

    def pos_arrival(q):
        return rcopy(pos, pos_all.at[q], s_pos.at[0], r_pos.at[q], other)

    def feat_copy(j):
        return rcopy(feats, feats_all.at[p], s_feat.at[j], r_feat.at[p], plane_dev(j))

    def feat_arrival(q):
        return rcopy(feats, feats_all.at[q], s_feat.at[0], r_feat.at[q], other)

    edge_pos = rcopy(pos, pos_all.at[plane], s_pos.at[0], r_pos.at[plane], edge)
    edge_feat = rcopy(feats, feats_all.at[plane], s_feat.at[0], r_feat.at[plane], edge)

    for j in range(1, nz):
        kv_copy(j).start()

    @pl.loop(1, plane)
    def _(j):
        pos_copy(j).start()

    @pl.loop(1, plane)
    def _(j):
        feat_copy(j).start()

    @pl.when(at_low | at_high)
    def _():
        edge_pos.start()
        edge_feat.start()

    def place_k(block, rows):
        k_cols[pl.ds(pl.multiple_of(block * kb, 8), kb), :] = columns(rows)[:kb]

    place_k(z, kv[...])
    if kpad > kall:
        k_cols[kall:, :] = jnp.zeros((kpad - kall, 128), F32)
    for j in range(1, nz):
        kv_arrival(j).wait_recv()
        q = (z + j) % nz
        place_k(q, kv_all[q])

    chunk = 32

    def phases(q, rows3):
        px, py, pz = rows3[0:1], rows3[1:2], rows3[2:3]
        lanes = rows_of(q)

        @pl.loop(0, kpad // chunk)
        def _(i):
            ks = pl.ds(pl.multiple_of(i * chunk, chunk), chunk)
            kc = k_cols[ks, :]
            s, c = sincos(kc[:, 0:1] * px + kc[:, 1:2] * py + kc[:, 2:3] * pz)
            a, b = split(c)
            ch[ks, lanes] = a
            cl[ks, lanes] = b
            a, b = split(s)
            sh[ks, lanes] = a
            sl[ks, lanes] = b

    def place_f(q, block):
        a, b = split(block)
        fbh[rows_of(q), :] = a
        fbl[rows_of(q), :] = b

    phases(p, pos[...])
    place_f(p, feats[...])

    @pl.loop(1, plane)
    def _(j):
        q = (p + j) % plane
        pos_arrival(q).wait_recv()
        phases(q, pos_all[q])

    @pl.loop(1, plane)
    def _(j):
        q = (p + j) % plane
        feat_arrival(q).wait_recv()
        place_f(q, feats_all[q])

    natoms = plane * slots

    def partial_sums(zb):
        ks = pl.ds(pl.multiple_of(zb * kb, 8), kb)
        f = (fbh[:natoms, :], fbl[:natoms, :])
        for part, (hi, lo) in enumerate(((ch, cl), (sh, sl))):
            total = dot3((hi[ks, :], lo[ks, :]), f)
            for h in range(2):
                s_acc[zb, h, part] = total[h * half : (h + 1) * half]

    def x_copy(zb):
        return rcopy(s_acc.at[zb, 1 - r], xbuf.at[zb], s_x.at[zb], r_x.at[zb], other)

    def z_copy(j):
        return rcopy(zs.at[j], zr.at[j], s_z.at[j], r_z.at[j], z_dev(j))

    def pass_on(j):
        zb = (z + j) % nz
        x_copy(zb).wait_recv()
        zs[j] = s_acc[zb, r] + xbuf[zb]
        if j:
            z_copy(j).start()

    order = sorted(range(nz), key=lambda j: -min(j, nz - j))
    for i, j in enumerate(order):
        zb = (z + j) % nz
        partial_sums(zb)
        x_copy(zb).start()
        if i:
            pass_on(order[i - 1])
    pass_on(order[-1])

    @pl.when(at_low | at_high)
    def _():
        edge_pos.wait_recv()
        edge_feat.wait_recv()
        place_f(plane, feats_all[plane])

    first = (r * waves + w) * cells
    total_cells = cells * waves * 2
    own_cols = columns(pos[...])
    low_slot = jnp.where(at_low, plane, p - 1)
    high_slot = jnp.where(at_high, plane, p + 1)
    same = lax.broadcasted_iota(jnp.int32, (slots, slots), 0) == lax.broadcasted_iota(
        jnp.int32, (slots, slots), 1
    )
    row_cell = lax.broadcasted_iota(jnp.int32, (slots, slots), 0) // cell
    col_cell = lax.broadcasted_iota(jnp.int32, (slots, slots), 1) // cell

    def listed(c, target):
        found = jnp.float32(0.0)
        for b in range(neigh.shape[1]):
            hit = (neigh[c, b] == target) & (b < ncount[c])
            found = found + jnp.where(hit, 1.0, 0.0)
        return found

    gathered = jnp.zeros((slots, width), F32)
    for shift, slot in ((-1, low_slot), (0, p), (1, high_slot)):
        near = pos[...] if shift == 0 else pos_all[slot]
        dist = jnp.zeros((slots, slots), F32)
        for axis in range(3):
            diff = own_cols[:, axis : axis + 1] - near[axis : axis + 1]
            dist = dist + diff * diff
        live = jnp.zeros((slots, slots), F32)
        for c in range(cells):
            for t in range(cells):
                target = (first + shift * cells + t + total_cells) % total_cells
                live = jnp.where((row_cell == c) & (col_cell == t), listed(c, target), live)
        weight = jnp.exp(-0.125 * dist) * live
        if shift == 0:
            weight = jnp.where(same, 0.0, weight)
        gathered = gathered + dot3(split(weight), (fbh[rows_of(slot), :], fbl[rows_of(slot), :]))
    msg[...] = feats[...] + 0.125 * dot3(split(gathered), split(w_msg[...]))

    total = zs[0]
    for j in range(1, nz):
        z_copy(j).wait_recv()
        total = total + zr[j]
    mine = pl.multiple_of(r * half, 8)
    wv = split(w_val[...])
    own_filter = filt[pl.ds(mine, half), :] * scale

    def share(zb, h):
        return f_all.at[:, pl.ds(pl.multiple_of((zb * 2 + h) * half, 8), half), :]

    for part in range(2):
        f_all[part, pl.ds(pl.multiple_of((z * 2 + r) * half, 8), half), :] = own_filter * dot3(
            split(total[part]), wv
        )
    if kpad > kall:
        f_all[:, kall:, :] = jnp.zeros((2, kpad - kall, width), F32)

    def f_copy(j):
        return rcopy(share(z, r), share(z, r), s_f.at[j], r_f.at[z, r], z_dev(j))

    def f_relay(zb):
        return rcopy(share(zb, r), share(zb, r), s_g.at[zb], r_f.at[zb, r], other)

    def f_arrival(zb, h):
        return rcopy(share(zb, h), share(zb, h), s_g.at[zb], r_f.at[zb, h], other)

    for j in order[:-1]:
        f_copy(j).start()
    f_relay(z).start()
    near_first = order[::-1][1:]
    for j in near_first:
        zb = (z + j) % nz
        f_arrival(zb, r).wait_recv()
        f_relay(zb).start()
    for j in [0] + near_first:
        f_arrival((z + j) % nz, 1 - r).wait_recv()
    for part in range(2):
        a, b = split(f_all[part].T)
        fth[part] = a
        ftl[part] = b

    def back(q):
        lanes = rows_of(q)
        return dot3((fth[0], ftl[0]), (ch[:, lanes], cl[:, lanes])) + dot3(
            (fth[1], ftl[1]), (sh[:, lanes], sl[:, lanes])
        )

    def e_copy(j):
        return rcopy(es.at[j], er.at[j], s_e.at[j], r_e.at[j], plane_dev(j))

    @pl.loop(1, plane)
    def _(j):
        es[j] = back((p + j) % plane)
        e_copy(j).start()

    es[0] = back(p)

    @pl.loop(1, plane)
    def _(j):
        e_copy(j).wait_recv()
        es[0] = es[0] + er[j]

    summed = msg[...] + es[0].T
    normed = summed / jnp.sqrt(jnp.mean(summed * summed, axis=1, keepdims=True) + 1e-06)
    v = dot3(split(normed), split(w_one[...]))
    hidden = v / (1.0 + jnp.exp(-v))
    result = summed + dot3(split(hidden), split(w_two[...]))
    slot_ids = lax.broadcasted_iota(jnp.int32, (cell, width), 0)
    for c in range(cells):
        out[c * cell : (c + 1) * cell, :] = jnp.where(
            slot_ids < counts[c], result[c * cell : (c + 1) * cell], 0.0
        )

    for j in range(1, nz):
        kv_copy(j).wait_send()
        z_copy(j).wait_send()
        f_copy(j).wait_send()
    for zb in range(nz):
        x_copy(zb).wait_send()
        f_relay(zb).wait_send()

    @pl.loop(1, plane)
    def _(j):
        pos_copy(j).wait_send()
        feat_copy(j).wait_send()
        e_copy(j).wait_send()

    @pl.when(at_low | at_high)
    def _():
        edge_pos.wait_send()
        edge_feat.wait_send()


def shards(
    nz, feats, positions, cell_counts, neighbours, nbr_count, kvec, filters, w_msg, w_val, w_one, w_two
):
    cells = cell_counts.shape[0]
    slots, width = feats.shape
    cell = slots // cells
    kb = kvec.shape[1]
    waves = lax.axis_size("waves")
    plane = waves // nz
    devices = lax.axis_size("rows") * waves
    kpad = -(-nz * kb // 128) * 128
    kbpad = -(-kb // 128) * 128
    half = kb // 2
    scale = 1.0 / math.sqrt(float(slots * devices) * float(kb * waves))
    slot_ids = jnp.arange(cell, dtype=jnp.int32)
    valid = (slot_ids[None, :] < cell_counts[:, None]).astype(F32).reshape(-1)
    masked = feats * valid[:, None]
    pos8 = jnp.pad(positions, ((0, 5), (0, 0)))
    kv8 = jnp.pad(kvec * (0.5 / math.pi), ((0, 5), (0, kbpad - kb)))
    natoms = plane * slots
    vm = pltpu.VMEM
    dma = pltpu.SemaphoreType.DMA
    smem_spec = pl.BlockSpec(memory_space=pltpu.SMEM)
    vmem_spec = pl.BlockSpec(memory_space=pltpu.VMEM)
    return pl.pallas_call(
        functools.partial(body, nz, plane, scale),
        out_shape=jax.ShapeDtypeStruct((slots, width), F32),
        in_specs=[smem_spec] * 3 + [vmem_spec] * 8,
        out_specs=vmem_spec,
        scratch_shapes=[
            vm((plane + 1, slots, width), F32),
            vm((plane + 1, 8, slots), F32),
            vm((nz, 8, kbpad), F32),
            vm((kpad, 128), F32),
            vm((kpad, natoms), BF16),
            vm((kpad, natoms), BF16),
            vm((kpad, natoms), BF16),
            vm((kpad, natoms), BF16),
            vm((natoms + slots, width), BF16),
            vm((natoms + slots, width), BF16),
            vm((nz, 2, 2, half, width), F32),
            vm((nz, 2, half, width), F32),
            vm((nz, 2, half, width), F32),
            vm((nz, 2, half, width), F32),
            vm((2, kpad, width), F32),
            vm((2, width, kpad), BF16),
            vm((2, width, kpad), BF16),
            vm((plane, width, slots), F32),
            vm((plane, width, slots), F32),
            vm((slots, width), F32),
            dma((plane,)),
            dma((plane + 1,)),
            dma((plane,)),
            dma((plane + 1,)),
            dma((nz,)),
            dma((nz,)),
            dma((nz,)),
            dma((nz,)),
            dma((nz,)),
            dma((nz,)),
            dma((nz,)),
            dma((nz, 2)),
            dma((nz,)),
            dma((plane,)),
            dma((plane,)),
        ],
        compiler_params=pltpu.CompilerParams(collective_id=0, has_side_effects=True),
        name="ewald_layer",
    )(cell_counts, neighbours, nbr_count, masked, pos8, kv8, filters, w_msg, w_val, w_one, w_two)


def solution(mesh):
    nz = 4 if mesh.shape["waves"] % 4 == 0 else 2
    placed = (
        P(("rows", "waves"), None),
        P(None, ("rows", "waves")),
        P(("rows", "waves")),
        P(("rows", "waves"), None),
        P(("rows", "waves")),
        P(None, "waves"),
        P("waves", None),
        P(),
        P(),
        P(),
        P(),
    )
    return jax.shard_map(
        functools.partial(shards, nz),
        mesh=mesh,
        in_specs=placed,
        out_specs=P(("rows", "waves"), None),
        check_vma=False,
    )
```

time: 305 us -> 90.9 us (0.30)
  the two profiles are of different devices: /device:TPU:0 before, /device:TPU:19 now
where the time goes in v1:
time: 90.9 us; the launch traced here: 90.6 us
  Pallas kernels  84.5 us (93%)
  other arithmetic  3.17 us (3%)
  local copies, waits for them, and re-layouts  2.96 us (3%)
    pallas_call x1, Pallas kernels, shards(): pl.pallas_call(functools.partial(body, nz, plane, scale), out_shape=jax.S...  84.5 us

profile of v1, /device:TPU:19, one launch (start us, length us, event | category | flops | bytes accessed | tf_op | source)
XLA Modules:
  0.0 90.6 jit_solution(10081884869014457197)
XLA Ops:
  0.0 0.7 fusion
  0.7 0.7 broadcast_multiply_fusion.1
  1.4 0.0 copy-start
  1.4 0.6 pad.9.kv
  2.0 0.1 copy-done
  2.1 0.6 pad.8.pos
  2.7 1.8 %broadcast_multiply_fusion.feats = f32[256,256]{1,0:T(8,128)} fusion(f32[256,256]{1,0:T(8,128)} %param.11, f32[256]{0:T(256)S(1)} %fusion), kind=kLoop, calls=%fused_computation | loop fusion | flops 65536 | bytes 525312 | tf_op jit(solution)/shard_map/mul | solution.py:377
  4.5 84.5 %ewald_layer.1 = f32[256,256]{1,0:T(8,128)} custom-call(s32[2]{0:T(128)} %counts.1, s32[2,5]{1,0:T(2,128)} %neigh.1, s32[2]{0:T(128)} %ncount.1, f32[256,256]{1,0:T(8,128)} %broadcast_multiply_fusion.feats, f32[8,256]{1,0:T(8,128)} %pad.8.pos, f32[8,256]{1,0:T(8,128)} %pad.9.kv, f32[192,256]{1,0:T(8,128)} %filt.1, f32[256,256]{1,0:T(8,128)} %w_msg.1, ...), custom_call_target="tpu_custom_call" | custom-call | tf_op jit(solution)/shard_map/ewald_layer/pallas_call | solution.py:385
  89.0 1.7 %copy.13 = f32[256,256]{1,0:T(8,128)} copy(f32[256,256]{1,0:T(8,128)} %ewald_layer.1) | data formatting | bytes 524288
Async XLA Ops:
  1.4 0.7 copy-start

commit v2 on v1

--- a/solution.py
+++ b/solution.py
@@ -203,19 +203,31 @@
     def x_copy(zb):
         return rcopy(s_acc.at[zb, 1 - r], xbuf.at[zb], s_x.at[zb], r_x.at[zb], other)
 
-    def z_copy(j):
-        return rcopy(zs.at[j], zr.at[j], s_z.at[j], r_z.at[j], z_dev(j))
-
-    def pass_on(j):
-        zb = (z + j) % nz
+    def step(up):
+        return z_dev(1) if up else z_dev(nz - 1)
+
+    def s_hop(zb, up):
+        side = 0 if up else 1
+        return rcopy(zs.at[zb], zr.at[side, zb], s_z.at[zb], r_z.at[side, zb], step(up))
+
+    def pass_on(zb):
         x_copy(zb).wait_recv()
-        zs[j] = s_acc[zb, r] + xbuf[zb]
-        if j:
-            z_copy(j).start()
-
-    order = sorted(range(nz), key=lambda j: -min(j, nz - j))
-    for i, j in enumerate(order):
-        zb = (z + j) % nz
+        zs[zb] = s_acc[zb, r] + xbuf[zb]
+        for up, ahead, behind in ((True, z < zb, z > 0), (False, z > zb, z < nz - 1)):
+
+            @pl.when(ahead & behind)
+            def _():
+                s_hop(zb, up).wait_recv()
+                zs[zb] = zs[zb] + zr[0 if up else 1, zb]
+
+            @pl.when(ahead)
+            def _():
+                s_hop(zb, up).start()
+
+    order = []
+    for i in range(nz // 2):
+        order += [nz - 1 - i, i]
+    for i, zb in enumerate(order):
         partial_sums(zb)
         x_copy(zb).start()
         if i:
@@ -264,70 +276,115 @@
         gathered = gathered + dot3(split(weight), (fbh[rows_of(slot), :], fbl[rows_of(slot), :]))
     msg[...] = feats[...] + 0.125 * dot3(split(gathered), split(w_msg[...]))
 
-    total = zs[0]
-    for j in range(1, nz):
-        z_copy(j).wait_recv()
-        total = total + zr[j]
+    for up, behind in ((True, z > 0), (False, z < nz - 1)):
+
+        @pl.when(behind)
+        def _():
+            s_hop(z, up).wait_recv()
+            zs[z] = zs[z] + zr[0 if up else 1, z]
+
+    total = zs[z]
     mine = pl.multiple_of(r * half, 8)
     wv = split(w_val[...])
     own_filter = filt[pl.ds(mine, half), :] * scale
 
-    def share(zb, h):
-        return f_all.at[:, pl.ds(pl.multiple_of((zb * 2 + h) * half, 8), half), :]
+    hw = width // 2
+
+    def share(fh, zb, h):
+        return f_all.at[fh, :, pl.ds(pl.multiple_of((zb * 2 + h) * half, 8), half), :]
 
     for part in range(2):
-        f_all[part, pl.ds(pl.multiple_of((z * 2 + r) * half, 8), half), :] = own_filter * dot3(
-            split(total[part]), wv
+        filtered = own_filter * dot3(split(total[part]), wv)
+        for fh in range(2):
+            f_all[fh, part, pl.ds(pl.multiple_of((z * 2 + r) * half, 8), half), :] = filtered[
+                :, fh * hw : (fh + 1) * hw
+            ]
+    if kpad > kall:
+        f_all[:, :, kall:, :] = jnp.zeros((2, 2, kpad - kall, hw), F32)
+
+    def f_hop(fh, zb, up, d):
+        here = share(fh, zb, r)
+        return rcopy(here, here, s_f.at[fh, int(up), d], r_f.at[fh, zb, r], step(up))
+
+    def f_relay(fh, zb):
+        here = share(fh, zb, r)
+        return rcopy(here, here, s_g.at[fh, zb], r_f.at[fh, zb, r], other)
+
+    def f_arrival(fh, zb, h):
+        here = share(fh, zb, h)
+        return rcopy(here, here, s_g.at[fh, zb], r_f.at[fh, zb, h], other)
+
+    def f_own(fh):
+        for up, ahead in ((True, z < nz - 1), (False, z > 0)):
+
+            @pl.when(ahead)
+            def _():
+                f_hop(fh, z, up, 0).start()
+
+        f_relay(fh, z).start()
+
+    def f_pass(fh, d):
+        for up, there, ahead in ((True, z >= d, z < nz - 1), (False, z + d < nz, z > 0)):
+            zb = z - d if up else z + d
+
+            @pl.when(there)
+            def _():
+                f_arrival(fh, zb, r).wait_recv()
+
+            @pl.when(there & ahead)
+            def _():
+                f_hop(fh, zb, up, d).start()
+
+            @pl.when(there)
+            def _():
+                f_relay(fh, zb).start()
+
+    def back(fh, q):
+        lanes = rows_of(q)
+        return dot3((fth[fh, 0], ftl[fh, 0]), (ch[:, lanes], cl[:, lanes])) + dot3(
+            (fth[fh, 1], ftl[fh, 1]), (sh[:, lanes], sl[:, lanes])
         )
-    if kpad > kall:
-        f_all[:, kall:, :] = jnp.zeros((2, kpad - kall, width), F32)
-
-    def f_copy(j):
-        return rcopy(share(z, r), share(z, r), s_f.at[j], r_f.at[z, r], z_dev(j))
-
-    def f_relay(zb):
-        return rcopy(share(zb, r), share(zb, r), s_g.at[zb], r_f.at[zb, r], other)
-
-    def f_arrival(zb, h):
-        return rcopy(share(zb, h), share(zb, h), s_g.at[zb], r_f.at[zb, h], other)
-
-    for j in order[:-1]:
-        f_copy(j).start()
-    f_relay(z).start()
-    near_first = order[::-1][1:]
-    for j in near_first:
-        zb = (z + j) % nz
-        f_arrival(zb, r).wait_recv()
-        f_relay(zb).start()
-    for j in [0] + near_first:
-        f_arrival((z + j) % nz, 1 - r).wait_recv()
-    for part in range(2):
-        a, b = split(f_all[part].T)
-        fth[part] = a
-        ftl[part] = b
-
-    def back(q):
-        lanes = rows_of(q)
-        return dot3((fth[0], ftl[0]), (ch[:, lanes], cl[:, lanes])) + dot3(
-            (fth[1], ftl[1]), (sh[:, lanes], sl[:, lanes])
-        )
-
-    def e_copy(j):
-        return rcopy(es.at[j], er.at[j], s_e.at[j], r_e.at[j], plane_dev(j))
-
-    @pl.loop(1, plane)
-    def _(j):
-        es[j] = back((p + j) % plane)
-        e_copy(j).start()
-
-    es[0] = back(p)
-
-    @pl.loop(1, plane)
-    def _(j):
-        e_copy(j).wait_recv()
-        es[0] = es[0] + er[j]
-
-    summed = msg[...] + es[0].T
+
+    def e_copy(fh, j):
+        return rcopy(es.at[fh, j], er.at[fh, j], s_e.at[fh, j], r_e.at[fh, j], plane_dev(j))
+
+    def gather_half(fh):
+        for zb in range(nz):
+            f_arrival(fh, zb, 1 - r).wait_recv()
+        for part in range(2):
+            a, b = split(f_all[fh, part].T)
+            fth[fh, part] = a
+            ftl[fh, part] = b
+
+    def back_range(fh, start, stop):
+        @pl.loop(start, stop)
+        def _(j):
+            es[fh, j] = back(fh, (p + j) % plane)
+            e_copy(fh, j).start()
+
+    f_own(0)
+    for d in range(1, nz):
+        f_pass(0, d)
+        if d == 1:
+            f_own(1)
+    gather_half(0)
+    cuts = [1 + d * (plane - 1) // (nz - 1) for d in range(nz)]
+    for d in range(1, nz):
+        f_pass(1, d)
+        back_range(0, cuts[d - 1], cuts[d])
+    gather_half(1)
+    back_range(1, 1, plane)
+    for fh in range(2):
+        es[fh, 0] = back(fh, p)
+
+    for fh in range(2):
+
+        @pl.loop(1, plane)
+        def _(j):
+            e_copy(fh, j).wait_recv()
+            es[fh, 0] = es[fh, 0] + er[fh, j]
+
+    summed = msg[...] + jnp.concatenate([es[0, 0].T, es[1, 0].T], axis=1)
     normed = summed / jnp.sqrt(jnp.mean(summed * summed, axis=1, keepdims=True) + 1e-06)
     v = dot3(split(normed), split(w_one[...]))
     hidden = v / (1.0 + jnp.exp(-v))
@@ -340,17 +397,30 @@
 
     for j in range(1, nz):
         kv_copy(j).wait_send()
-        z_copy(j).wait_send()
-        f_copy(j).wait_send()
     for zb in range(nz):
         x_copy(zb).wait_send()
-        f_relay(zb).wait_send()
+        for up, ahead in ((True, z < zb), (False, z > zb)):
+
+            @pl.when(ahead)
+            def _():
+                s_hop(zb, up).wait_send()
+
+        for fh in range(2):
+            f_relay(fh, zb).wait_send()
+    for fh in range(2):
+        for d in range(nz):
+            for up, there, ahead in ((True, z >= d, z < nz - 1), (False, z + d < nz, z > 0)):
+
+                @pl.when(there & ahead)
+                def _():
+                    f_hop(fh, z - d if up else z + d, up, d).wait_send()
 
     @pl.loop(1, plane)
     def _(j):
         pos_copy(j).wait_send()
         feat_copy(j).wait_send()
-        e_copy(j).wait_send()
+        for fh in range(2):
+            e_copy(fh, j).wait_send()
 
     @pl.when(at_low | at_high)
     def _():
@@ -401,12 +471,12 @@
             vm((nz, 2, 2, half, width), F32),
             vm((nz, 2, half, width), F32),
             vm((nz, 2, half, width), F32),
-            vm((nz, 2, half, width), F32),
-            vm((2, kpad, width), F32),
-            vm((2, width, kpad), BF16),
-            vm((2, width, kpad), BF16),
-            vm((plane, width, slots), F32),
-            vm((plane, width, slots), F32),
+            vm((2, nz, 2, half, width), F32),
+            vm((2, 2, kpad, width // 2), F32),
+            vm((2, 2, width // 2, kpad), BF16),
+            vm((2, 2, width // 2, kpad), BF16),
+            vm((2, plane, width // 2, slots), F32),
+            vm((2, plane, width // 2, slots), F32),
             vm((slots, width), F32),
             dma((plane,)),
             dma((plane + 1,)),
@@ -417,12 +487,12 @@
             dma((nz,)),
             dma((nz,)),
             dma((nz,)),
-            dma((nz,)),
-            dma((nz,)),
-            dma((nz, 2)),
-            dma((nz,)),
-            dma((plane,)),
-            dma((plane,)),
+            dma((2, nz)),
+            dma((2, 2, nz)),
+            dma((2, nz, 2)),
+            dma((2, nz)),
+            dma((2, plane)),
+            dma((2, plane)),
         ],
         compiler_params=pltpu.CompilerParams(collective_id=0, has_side_effects=True),
         name="ewald_layer",

time: 90.9 us -> 88.6 us (0.975)
  the two profiles are of different devices: /device:TPU:19 before, /device:TPU:0 now
where the time goes in v2:
time: 88.6 us; the launch traced here: 88.4 us
  Pallas kernels  82.2 us (93%)
  other arithmetic  3.17 us (4%)
  local copies, waits for them, and re-layouts  2.96 us (3%)
    pallas_call x1, Pallas kernels, shards(): pl.pallas_call(functools.partial(body, nz, plane, scale), out_shape=jax.S...  82.2 us

profile of v2, /device:TPU:0, one launch (start us, length us, event | category | flops | bytes accessed | tf_op | source)
XLA Modules:
  0.0 88.4 jit_solution(4633273972062271379)
XLA Ops:
  0.0 0.7 fusion
  0.7 0.7 broadcast_multiply_fusion.1
  1.4 0.0 copy-start
  1.4 0.6 pad.9.kv
  2.0 0.1 copy-done
  2.1 0.6 pad.8.pos
  2.7 1.8 %broadcast_multiply_fusion.feats = f32[256,256]{1,0:T(8,128)} fusion(f32[256,256]{1,0:T(8,128)} %param.11, f32[256]{0:T(256)S(1)} %fusion), kind=kLoop, calls=%fused_computation | loop fusion | flops 65536 | bytes 525312 | tf_op jit(solution)/shard_map/mul | solution.py:447
  4.5 82.2 %ewald_layer.1 = f32[256,256]{1,0:T(8,128)} custom-call(s32[2]{0:T(128)} %counts.1, s32[2,5]{1,0:T(2,128)} %neigh.1, s32[2]{0:T(128)} %ncount.1, f32[256,256]{1,0:T(8,128)} %broadcast_multiply_fusion.feats, f32[8,256]{1,0:T(8,128)} %pad.8.pos, f32[8,256]{1,0:T(8,128)} %pad.9.kv, f32[192,256]{1,0:T(8,128)} %filt.1, f32[256,256]{1,0:T(8,128)} %w_msg.1, ...), custom_call_target="tpu_custom_call" | custom-call | tf_op jit(solution)/shard_map/ewald_layer/pallas_call | solution.py:455
  86.7 1.7 %copy.13 = f32[256,256]{1,0:T(8,128)} copy(f32[256,256]{1,0:T(8,128)} %ewald_layer.1) | data formatting | bytes 524288
Async XLA Ops:
  1.4 0.7 copy-start
